TPU v7x, 32 devices: a whole 2x2x4 slice. The times are simulated.
32 devices in a mesh: img: 2 (over x), sp: 2 (over core), tp: 8 (over z, y).
Axes of the slice: x: 2, y: 2, z: 4, core: 2. Of those that a mesh axis runs over, the one named last changes fastest.
Arguments:
- tokens: bfloat16 [16, 32, 6144], P(('img', 'tp'), 'sp'), parts along dimension 0, may hold values from -6 to 6
- up_weight: bfloat16 [6144, 24576], P('sp', 'tp'), may hold values from -0.078125 to 0.078125
- up_bias: float32 [24576], P('tp'), may hold values from -3 to 3
- conv_weight: float32 [3, 3, 24576], P(None, None, 'tp'), may hold values from -2 to 2
- conv_bias: float32 [24576], P('tp'), may hold values from -3 to 3
- down_weight: bfloat16 [24576, 6144], P('tp', 'sp'), may hold values from -0.0390625 to 0.0390625
- down_bias: float32 [6144], replicated, may hold values from -3 to 3
Outputs:
- projected: bfloat16 [16, 32, 6144], P(('img', 'tp'), 'sp'), parts along dimension 0
There are 2 independent parts, one for each index of `img`. A program takes and returns all parts, laid end to end along the dimension named above; an argument that names none is the same for every part. Nothing has to cross between parts.
All inputs are finite; a program needn't handle non-finite values.
Results may differ from a plain program's by a relative error of at most 0.0053.
Values may be sent and summed in bfloat16 or wider, within the bound.
No kernel may reach another device: no remote copies, remote signals or barrier semaphores. Data moves between devices by JAX's collectives and lax.ppermute only.
A program may use at most 256 MiB of HBM per device.

v0:
```python
import jax
import jax.numpy as jnp
from jax import lax
from jax.sharding import PartitionSpec as P


def extended(block, sides, width):
    for axis, dim in sides:
        count = lax.axis_size(axis)
        forward = [(i, i + 1) for i in range(count - 1)]
        backward = [(target, source) for source, target in forward]
        low = lax.ppermute(
            lax.slice_in_dim(block, block.shape[dim] - width, None, axis=dim), axis, forward
        )
        high = lax.ppermute(lax.slice_in_dim(block, 0, width, axis=dim), axis, backward)
        block = jnp.concatenate([low, block, high], axis=dim)
    return block


def depthwise(hidden, conv_weight, conv_bias):
    padded = extended(hidden, (("sp", 1),), 1)
    padded = jnp.pad(padded, ((1, 1), (0, 0), (0, 0)))
    extent_x = hidden.shape[0]
    extent_y = hidden.shape[1]
    summed = jnp.zeros(hidden.shape, jnp.float32) + conv_bias
    for offset_x in range(3):
        for offset_y in range(3):
            window = padded[offset_x : offset_x + extent_x, offset_y : offset_y + extent_y]
            summed = summed + window.astype(jnp.float32) * conv_weight[offset_x, offset_y]
    return jax.nn.gelu(summed, approximate=False).astype(jnp.bfloat16)


def local(tokens, up_weight, up_bias, conv_weight, conv_bias, down_weight, down_bias):
    col_count = tokens.shape[0]
    row_count = tokens.shape[1]
    width_model = tokens.shape[2]
    hidden_dev = up_weight.shape[1]
    up_full, down_full = (
        lax.all_gather(up_weight, "sp", axis=0, tiled=True),
        lax.all_gather(down_weight, "sp", axis=1, tiled=True),
    )
    piece = lax.all_gather(tokens, "tp", axis=0, tiled=True)
    flat_piece = piece.reshape(-1, width_model)
    lifted = jnp.dot(flat_piece, up_full, preferred_element_type=jnp.float32) + up_bias
    hidden = lifted.astype(jnp.bfloat16).reshape(piece.shape[0], row_count, hidden_dev)
    mixed = depthwise(hidden, conv_weight, conv_bias)
    product = jnp.dot(mixed.reshape(-1, hidden_dev), down_full, preferred_element_type=jnp.float32)
    summed_terms = lax.psum_scatter(
        product.reshape(col_count * lax.axis_size("tp"), row_count, width_model),
        "tp",
        scatter_dimension=0,
        tiled=True,
    )
    return (summed_terms + down_bias).astype(jnp.bfloat16)


def solution(mesh):
    placed = (
        P(("img", "tp"), "sp", None),
        P("sp", "tp"),
        P("tp"),
        P(None, None, "tp"),
        P("tp"),
        P("tp", "sp"),
        P(),
    )
    return jax.shard_map(
        local, mesh=mesh, in_specs=placed, out_specs=P(("img", "tp"), "sp", None), check_vma=False
    )
```

profile of v0, /device:TPU:0, one launch (start us, length us, event | category | flops | bytes accessed | tf_op | source)
XLA Modules:
  0.0 277.0 jit_solution(13013426997348441983)
XLA Ops:
  6.5 0.7 all-gather.4.cloned.1.call-update
  7.3 0.0 all-gather.6.cloned.1.call-start
  7.3 0.7 all-gather.6.cloned.1.call-update
  8.0 0.0 copy-start.2
  8.0 0.0 all-gather.8.cloned.1.call-start
  8.1 0.7 all-gather.8.cloned.1.call-update
  8.8 0.0 reduce-scatter.2.cloned.1.call-start
  8.8 47.7 %all-gather.4.cloned.1.call-done = bf16[8,16,6144]{2,1,0:T(8,128)(2,1)} async-done(((bf16[1,16,6144]{2,1,0:T(8,128)(2,1)}), bf16[8,16,6144]{2,1,0:T(8,128)(2,1)}) %all-gather.4.cloned.1.call-update) | async-done | bytes 1572880 | tf_op jit(solution)/shard_map/all_gather | solution.py:42
  56.5 58.2 %all-gather.6.cloned.1.call-done = bf16[6144,3072]{1,0:T(8,128)(2,1)} async-done(((bf16[3072,3072]{1,0:T(8,128)(2,1)}), bf16[6144,3072]{1,0:T(8,128)(2,1)}) %all-gather.6.cloned.1.call-update) | async-done | bytes 37748752 | tf_op jit(solution)/shard_map/all_gather | solution.py:39
  114.7 18.7 %fusion.2 = bf16[128,3072]{1,0:T(8,128)(2,1)S(1)} fusion(bf16[128,6144]{1,0:T(8,128)(2,1)} %bitcast.19, bf16[6144,3072]{1,0:T(8,128)(2,1)} %all-gather.6.cloned.1.call-done, f32[3072]{0:T(1024)S(1)} %copy-done.2), kind=kOutput, calls=%fused_computation.5 | convolution fusion | flops 4832624640 | bytes 40120320 | tf_op jit(solution)/shard_map/dot_general | solution.py:44
  133.3 0.0 copy-start.3
  133.3 0.2 fusion.99
  133.5 2.0 collective-permute-start
  135.5 1.3 collective-permute-start.1
  136.8 0.0 copy-done
  136.8 0.1 fusion.100
  136.9 0.0 collective-permute-done
  136.9 1.8 collective-permute-done.1
  138.7 0.5 fusion.18
  139.2 36.0 %all-gather.8.cloned.1.call-done = bf16[3072,6144]{1,0:T(8,128)(2,1)} async-done(((bf16[3072,3072]{1,0:T(8,128)(2,1)}), bf16[3072,6144]{1,0:T(8,128)(2,1)}) %all-gather.8.cloned.1.call-update) | async-done | bytes 37748752 | tf_op jit(solution)/shard_map/all_gather | solution.py:40
  175.2 18.0 %fusion = f32[8,16,6144]{2,1,0:T(8,128)} fusion(bf16[3072,6144]{1,0:T(8,128)(2,1)} %all-gather.8.cloned.1.call-done, bf16[8,16,3072]{2,1,0:T(8,128)(2,1)S(1)} %bitcast.18, bf16[10,18,3072]{2,1,0:T(8,128)(2,1)S(1)} %fusion.18, bf16[8,1,3072]{2,1,0:T(2,128)(2,1)S(1)} %collective-permute-done.1, bf16[8,1,3072]{2,1,0:T(2,128)(2,1)S(1)} %collective-permute-done, ...), kind=kOutput, calls=%fused_computation | convolution fusion | flops 4870373376 | bytes 46718976 | tf_op jit(solution)/shard_map/dot_general | solution.py:47
  193.1 0.0 reduce-scatter.2.cloned.1.call-update
  193.2 75.6 %reduce-scatter.2.cloned.1.call-done = f32[1,16,6144]{2,1,0:T(8,128)} async-done(((f32[8,16,6144]{2,1,0:T(8,128)}), f32[1,16,6144]{2,1,0:T(8,128)}) %reduce-scatter.2.cloned.1.call-update) | async-done | bytes 393232 | tf_op jit(solution)/shard_map/reduce_scatter | solution.py:48
  268.7 1.7 add_convert_fusion
  (6 shorter events, 0.0 us)
Async XLA Ops:
  6.5 49.9 %all-gather.4.cloned.1.call-start = ((), (), s32[]{:S(2)}) async-start(), calls=%async_computation.1 | async-start | bytes 1769472 | tf_op jit(solution)/shard_map/all_gather | solution.py:42
  7.3 107.4 %all-gather.6.cloned.1.call-start = ((), (), s32[]{:S(2)}) async-start(), calls=%async_computation.2 | async-start | bytes 56623104 | tf_op jit(solution)/shard_map/all_gather | solution.py:39
  8.0 106.7 %copy-start.2 = (f32[3072]{0:T(1024)S(1)}, f32[3072]{0:T(1024)}, u32[]{:S(2)}) copy-start(f32[3072]{0:T(1024)} %param.9) | copy-start | bytes 36868
  8.0 167.2 %all-gather.8.cloned.1.call-start = ((), (), s32[]{:S(2)}) async-start(), calls=%async_computation.3 | async-start | bytes 56623104 | tf_op jit(solution)/shard_map/all_gather | solution.py:40
  8.8 260.0 %reduce-scatter.2.cloned.1.call-start = ((), (), s32[]{:S(2)}) async-start(), calls=%async_computation.4 | async-start | bytes 3538944 | tf_op jit(solution)/shard_map/reduce_scatter | solution.py:48
  114.7 22.1 %copy-start = (f32[3,3,3072]{2,1,0:T(4,128)S(1)}, f32[3,3,3072]{2,1,0:T(4,128)}, u32[]{:S(2)}) copy-start(f32[3,3,3072]{2,1,0:T(4,128)} %param.10) | copy-start | bytes 331780
  133.3 41.8 %copy-start.3 = (f32[3072]{0:T(1024)S(1)}, f32[3072]{0:T(1024)}, u32[]{:S(2)}) copy-start(f32[3072]{0:T(1024)} %param.11) | copy-start | bytes 36868
  133.5 3.4 %collective-permute-start = (bf16[8,1,3072]{2,1,0:T(2,128)(2,1)S(1)}, bf16[8,1,3072]{2,1,0:T(2,128)(2,1)S(1)}, u32[]{:S(2)}, u32[]{:S(2)}) collective-permute-start(bf16[8,1,3072]{2,1,0:T(2,128)(2,1)S(1)} %get-tuple-element.5), channel_id=1, source_target_pairs={{0,8},{1,9},{2,10},{3,11},{4,12},{5,13},{6,14},{7,15},{16,24},{17,... | collective-permute-start | bytes 147464 | tf_op jit(solution)/shard_map/ppermute | solution.py:12
  135.5 3.2 %collective-permute-start.1 = (bf16[8,1,3072]{2,1,0:T(2,128)(2,1)S(1)}, bf16[8,1,3072]{2,1,0:T(2,128)(2,1)S(1)}, u32[]{:S(2)}, u32[]{:S(2)}) collective-permute-start(bf16[8,1,3072]{2,1,0:T(2,128)(2,1)S(1)} %get-tuple-element.6), channel_id=1, source_target_pairs={{8,0},{9,1},{10,2},{11,3},{12,4},{13,5},{14,6},{15,7},{24,16},{25,... | collective-permute-start | bytes 147464 | tf_op jit(solution)/shard_map/ppermute | solution.py:15
  193.1 75.6 %copy-start.1 = (f32[6144]{0:T(1024)S(1)}, f32[6144]{0:T(1024)}, u32[]{:S(2)}) copy-start(f32[6144]{0:T(1024)} %param.13) | copy-start | bytes 73732
Sparse Core Ops, SparseCore 0:
  9.5 46.8 all-gather.3
  58.0 56.5 all-gather.5
  116.2 58.9 all-gather.7
  193.3 75.3 reduce-scatter.1
where the time goes:
time: 277 us
  waiting for transfers between devices  221 us (80%)
  matrix products  36.6 us (13%)
  between operations  13.2 us (5%)
  starting transfers between devices  3.38 us (1%)
    reduce_scatter x1, waiting for transfers between devices, local(): lax.psum_scatter(product.reshape(col_count * lax.axis_size('tp'), row_cou...  75.6 us
    all_gather x1, waiting for transfers between devices, local(): lax.all_gather(up_weight, 'sp', axis=0, tiled=True)  58.2 us
    all_gather x1, waiting for transfers between devices, local(): piece = lax.all_gather(tokens, 'tp', axis=0, tiled=True)  47.7 us
    all_gather x1, waiting for transfers between devices, local(): lax.all_gather(down_weight, 'sp', axis=1, tiled=True)  36 us
    dot_general x1, matrix products, local(): jnp.dot(flat_piece, up_full, preferred_element_type=jnp.float32) + up_bias  18.7 us
    dot_general x1, matrix products, local(): jnp.dot(mixed.reshape(-1, hidden_dev), down_full, preferred_element_type=...  18 us
  transfers between devices with their start and end apart: 6, of which 5 were waited for; matrix products, arithmetic and copies ran while one was open for 7% of the time, Pallas kernels for 0%

commit v1 on v0

--- a/solution.py
+++ b/solution.py
@@ -2,6 +2,24 @@
 import jax.numpy as jnp
 from jax import lax
 from jax.sharding import PartitionSpec as P
+
+
+def ring_gather(shard, axis, dim):
+    ways, here, step = (lax.axis_size(axis), lax.axis_index(axis), shard.shape[dim])
+    shape = [n * ways if d == dim else n for d, n in enumerate(shard.shape)]
+    full = lax.dynamic_update_slice_in_dim(
+        jnp.zeros(shape, shard.dtype), shard, here * step, axis=dim
+    )
+    going_up = going_down = shard
+    for far in range(1, ways // 2 + 1):
+        going_up = lax.ppermute(going_up, axis, [(d, (d + 1) % ways) for d in range(ways)])
+        full = lax.dynamic_update_slice_in_dim(full, going_up, (here - far) % ways * step, axis=dim)
+        if 2 * far < ways:
+            going_down = lax.ppermute(going_down, axis, [(d, (d - 1) % ways) for d in range(ways)])
+            full = lax.dynamic_update_slice_in_dim(
+                full, going_down, (here + far) % ways * step, axis=dim
+            )
+    return full
 
 
 def extended(block, sides, width):
@@ -39,7 +57,7 @@
         lax.all_gather(up_weight, "sp", axis=0, tiled=True),
         lax.all_gather(down_weight, "sp", axis=1, tiled=True),
     )
-    piece = lax.all_gather(tokens, "tp", axis=0, tiled=True)
+    piece = ring_gather(tokens, "tp", 0)
     flat_piece = piece.reshape(-1, width_model)
     lifted = jnp.dot(flat_piece, up_full, preferred_element_type=jnp.float32) + up_bias
     hidden = lifted.astype(jnp.bfloat16).reshape(piece.shape[0], row_count, hidden_dev)

time: 277 us -> 232 us (0.84)
  waiting for transfers between devices: 221 us -> 157 us
  starting transfers between devices: 3.38 us -> 22.8 us
    all_gather x1 -> x0, waiting for transfers between devices: 47.7 us -> none  [local(): piece = lax.all_gather(tokens, 'tp', axis=0, tiled=True)]
    all_gather x1, waiting for transfers between devices: 58.2 us -> 19.2 us  [local(): lax.all_gather(up_weight, 'sp', axis=0, tiled=True)]
    ppermute x0 -> x7, waiting for transfers between devices: none -> 22.1 us  [the longest x4 20.2 us: ring_gather(): lax.ppermute(going_up, axis, [(d, (d + 1) % ways) for d in range(ways)])]
    ppermute x0 -> x7, starting transfers between devices: none -> 19.5 us  [the longest x3 10.5 us: ring_gather(): lax.ppermute(going_down, axis, [(d, (d - 1) % ways) for d in range(ways)])]
  transfers between devices with their start and end apart: 6 -> 12, of which waited for: 5 -> 9; matrix products, arithmetic and copies ran while one was open for 7% -> 8% of each run, Pallas kernels for 0% -> 0%
where the time goes in v1:
time: 232 us
  waiting for transfers between devices  157 us (68%)
  matrix products  35.8 us (15%)
  starting transfers between devices  22.8 us (10%)
  between operations  13.4 us (6%)
    reduce_scatter x1, waiting for transfers between devices, local(): lax.psum_scatter(product.reshape(col_count * lax.axis_size('tp'), row_cou...  75.6 us
    all_gather x1, waiting for transfers between devices, local(): lax.all_gather(down_weight, 'sp', axis=1, tiled=True)  36.8 us
    ppermute x4, waiting for transfers between devices, ring_gather(): lax.ppermute(going_up, axis, [(d, (d + 1) % ways) for d in range(ways)])  20.2 us
    all_gather x1, waiting for transfers between devices, local(): lax.all_gather(up_weight, 'sp', axis=0, tiled=True)  19.2 us
    dot_general x1, matrix products, local(): jnp.dot(mixed.reshape(-1, hidden_dev), down_full, preferred_element_type=...  18 us
    dot_general x1, matrix products, local(): jnp.dot(flat_piece, up_full, preferred_element_type=jnp.float32) + up_bias  17.8 us
    ppermute x3, starting transfers between devices, ring_gather(): lax.ppermute(going_down, axis, [(d, (d - 1) % ways) for d in range(ways)])  10.5 us
    ppermute x4, starting transfers between devices, ring_gather(): lax.ppermute(going_up, axis, [(d, (d + 1) % ways) for d in range(ways)])  9.03 us
  transfers between devices with their start and end apart: 12, of which 9 were waited for; matrix products, arithmetic and copies ran while one was open for 8% of the time, Pallas kernels for 0%

profile of v1, /device:TPU:0, one launch (start us, length us, event | category | flops | bytes accessed | tf_op | source)
XLA Modules:
  0.0 231.8 jit_solution(2769930759722239279)
XLA Ops:
  6.5 0.7 all-gather.3.cloned.1.call-update
  7.3 0.7 all-gather.5.cloned.1.call-update
  8.2 3.0 %collective-permute-start = (bf16[1,16,6144]{2,1,0:T(8,128)(2,1)S(1)}, bf16[1,16,6144]{2,1,0:T(8,128)(2,1)S(1)}, u32[]{:S(2)}, u32[]{:S(2)}) collective-permute-start(bf16[1,16,6144]{2,1,0:T(8,128)(2,1)S(1)} %copy-done), channel_id=1, source_target_pairs={{0,1},{1,2},{2,3},{3,4},{4,5},{5,6},{6,7},{7,0},{8,9},{9,10},{10,1... | collective-permute-start | bytes 589832 | tf_op jit(solution)/shard_map/ppermute | solution.py:15
  11.2 3.0 %collective-permute-start.1 = (bf16[1,16,6144]{2,1,0:T(8,128)(2,1)S(1)}, bf16[1,16,6144]{2,1,0:T(8,128)(2,1)S(1)}, u32[]{:S(2)}, u32[]{:S(2)}) collective-permute-start(bf16[1,16,6144]{2,1,0:T(8,128)(2,1)S(1)} %copy-done), channel_id=1, source_target_pairs={{0,7},{1,0},{2,1},{3,2},{4,3},{5,4},{6,5},{7,6},{8,15},{9,8},{10,9... | collective-permute-start | bytes 589832 | tf_op jit(solution)/shard_map/ppermute | solution.py:18
  14.5 5.0 %collective-permute-done = bf16[1,16,6144]{2,1,0:T(8,128)(2,1)S(1)} collective-permute-done((bf16[1,16,6144]{2,1,0:T(8,128)(2,1)S(1)}, bf16[1,16,6144]{2,1,0:T(8,128)(2,1)S(1)}, u32[]{:S(2)}, u32[]{:S(2)}) %collective-permute-start) | collective-permute-done | bytes 196640 | tf_op jit(solution)/shard_map/ppermute | solution.py:15
  19.5 2.5 %collective-permute-start.2 = (bf16[1,16,6144]{2,1,0:T(8,128)(2,1)S(1)}, bf16[1,16,6144]{2,1,0:T(8,128)(2,1)S(1)}, u32[]{:S(2)}, u32[]{:S(2)}) collective-permute-start(bf16[1,16,6144]{2,1,0:T(8,128)(2,1)S(1)} %collective-permute-done), channel_id=1, source_target_pairs={{0,1},{1,2},{2,3},{3,4},{4,5},{5,6},{6,7},{7,0},{8,9},{9,10},{10,1... | collective-permute-start | bytes 589832 | tf_op jit(solution)/shard_map/ppermute | solution.py:15
  22.0 3.0 %collective-permute-start.3 = (bf16[1,16,6144]{2,1,0:T(8,128)(2,1)S(1)}, bf16[1,16,6144]{2,1,0:T(8,128)(2,1)S(1)}, u32[]{:S(2)}, u32[]{:S(2)}) collective-permute-start(bf16[1,16,6144]{2,1,0:T(8,128)(2,1)S(1)} %collective-permute-done.1), channel_id=1, source_target_pairs={{0,7},{1,0},{2,1},{3,2},{4,3},{5,4},{6,5},{7,6},{8,15},{9,8},{10,9... | collective-permute-start | bytes 589832 | tf_op jit(solution)/shard_map/ppermute | solution.py:18
  25.1 4.4 %collective-permute-done.2 = bf16[1,16,6144]{2,1,0:T(8,128)(2,1)S(1)} collective-permute-done((bf16[1,16,6144]{2,1,0:T(8,128)(2,1)S(1)}, bf16[1,16,6144]{2,1,0:T(8,128)(2,1)S(1)}, u32[]{:S(2)}, u32[]{:S(2)}) %collective-permute-start.2) | collective-permute-done | bytes 196640 | tf_op jit(solution)/shard_map/ppermute | solution.py:15
  29.5 2.5 %collective-permute-start.4 = (bf16[1,16,6144]{2,1,0:T(8,128)(2,1)S(1)}, bf16[1,16,6144]{2,1,0:T(8,128)(2,1)S(1)}, u32[]{:S(2)}, u32[]{:S(2)}) collective-permute-start(bf16[1,16,6144]{2,1,0:T(8,128)(2,1)S(1)} %collective-permute-done.2), channel_id=1, source_target_pairs={{0,1},{1,2},{2,3},{3,4},{4,5},{5,6},{6,7},{7,0},{8,9},{9,10},{10,1... | collective-permute-start | bytes 589832 | tf_op jit(solution)/shard_map/ppermute | solution.py:15
  32.0 4.4 %collective-permute-start.5 = (bf16[1,16,6144]{2,1,0:T(8,128)(2,1)S(1)}, bf16[1,16,6144]{2,1,0:T(8,128)(2,1)S(1)}, u32[]{:S(2)}, u32[]{:S(2)}) collective-permute-start(bf16[1,16,6144]{2,1,0:T(8,128)(2,1)S(1)} %collective-permute-done.3), channel_id=1, source_target_pairs={{0,7},{1,0},{2,1},{3,2},{4,3},{5,4},{6,5},{7,6},{8,15},{9,8},{10,9... | collective-permute-start | bytes 589832 | tf_op jit(solution)/shard_map/ppermute | solution.py:18
  36.4 3.7 %collective-permute-done.4 = bf16[1,16,6144]{2,1,0:T(8,128)(2,1)S(1)} collective-permute-done((bf16[1,16,6144]{2,1,0:T(8,128)(2,1)S(1)}, bf16[1,16,6144]{2,1,0:T(8,128)(2,1)S(1)}, u32[]{:S(2)}, u32[]{:S(2)}) %collective-permute-start.4) | collective-permute-done | bytes 196640 | tf_op jit(solution)/shard_map/ppermute | solution.py:15
  40.1 1.1 collective-permute-start.6
  41.2 2.0 collective-permute-done.5
  43.2 7.0 %collective-permute-done.6 = bf16[1,16,6144]{2,1,0:T(8,128)(2,1)S(1)} collective-permute-done((bf16[1,16,6144]{2,1,0:T(8,128)(2,1)S(1)}, bf16[1,16,6144]{2,1,0:T(8,128)(2,1)S(1)}, u32[]{:S(2)}, u32[]{:S(2)}) %collective-permute-start.6) | collective-permute-done | bytes 196640 | tf_op jit(solution)/shard_map/ppermute | solution.py:15
  50.3 19.2 %all-gather.3.cloned.1.call-done = bf16[6144,3072]{1,0:T(8,128)(2,1)} async-done(((bf16[3072,3072]{1,0:T(8,128)(2,1)}), bf16[6144,3072]{1,0:T(8,128)(2,1)}) %all-gather.3.cloned.1.call-update) | async-done | bytes 37748752 | tf_op jit(solution)/shard_map/all_gather | solution.py:57
  69.5 17.8 %fusion.2 = bf16[128,3072]{1,0:T(8,128)(2,1)S(1)} fusion(bf16[128,6144]{1,0:T(8,128)(2,1)S(1)} %bitcast.16, bf16[6144,3072]{1,0:T(8,128)(2,1)} %all-gather.3.cloned.1.call-done, f32[3072]{0:T(1024)S(1)} %copy-done.3), kind=kOutput, calls=%fused_computation.5 | convolution fusion | flops 4832624640 | bytes 40120320 | tf_op jit(solution)/shard_map/dot_general | solution.py:62
  87.5 2.0 collective-permute-start.7
  89.4 1.3 collective-permute-start.8
  90.9 1.8 collective-permute-done.8
  92.6 0.5 fusion.18
  93.1 36.8 %all-gather.5.cloned.1.call-done = bf16[3072,6144]{1,0:T(8,128)(2,1)} async-done(((bf16[3072,3072]{1,0:T(8,128)(2,1)}), bf16[3072,6144]{1,0:T(8,128)(2,1)}) %all-gather.5.cloned.1.call-update) | async-done | bytes 37748752 | tf_op jit(solution)/shard_map/all_gather | solution.py:58
  130.0 18.0 %fusion = f32[8,16,6144]{2,1,0:T(8,128)} fusion(bf16[3072,6144]{1,0:T(8,128)(2,1)} %all-gather.5.cloned.1.call-done, bf16[8,16,3072]{2,1,0:T(8,128)(2,1)S(1)} %bitcast.19, bf16[10,18,3072]{2,1,0:T(8,128)(2,1)S(1)} %fusion.18, bf16[8,1,3072]{2,1,0:T(2,128)(2,1)S(1)} %collective-permute-done.8, bf16[8,1,3072]{2,1,0:T(2,128)(2,1)S(1)} %collective-permute-done.7, ...), kind=kOutput, calls=%fused_computation | convolution fusion | flops 4870373376 | bytes 46718976 | tf_op jit(solution)/shard_map/dot_general | solution.py:65
  148.0 75.6 %reduce-scatter.2.cloned.1.call-done = f32[1,16,6144]{2,1,0:T(8,128)} async-done(((f32[8,16,6144]{2,1,0:T(8,128)}), f32[1,16,6144]{2,1,0:T(8,128)}) %reduce-scatter.2.cloned.1.call-update) | async-done | bytes 393232 | tf_op jit(solution)/shard_map/reduce_scatter | solution.py:66
  223.6 1.7 add_convert_fusion
  (28 shorter events, 0.8 us)
Async XLA Ops:
  6.5 62.9 %all-gather.3.cloned.1.call-start = ((), (), s32[]{:S(2)}) async-start(), calls=%async_computation.1 | async-start | bytes 56623104 | tf_op jit(solution)/shard_map/all_gather | solution.py:57
  7.3 0.9 copy-start
  7.3 122.7 %all-gather.5.cloned.1.call-start = ((), (), s32[]{:S(2)}) async-start(), calls=%async_computation.2 | async-start | bytes 56623104 | tf_op jit(solution)/shard_map/all_gather | solution.py:58
  8.0 215.5 %reduce-scatter.2.cloned.1.call-start = ((), (), s32[]{:S(2)}) async-start(), calls=%async_computation.3 | async-start | bytes 3538944 | tf_op jit(solution)/shard_map/reduce_scatter | solution.py:66
  8.2 11.3 %collective-permute-start = (bf16[1,16,6144]{2,1,0:T(8,128)(2,1)S(1)}, bf16[1,16,6144]{2,1,0:T(8,128)(2,1)S(1)}, u32[]{:S(2)}, u32[]{:S(2)}) collective-permute-start(bf16[1,16,6144]{2,1,0:T(8,128)(2,1)S(1)} %copy-done), channel_id=1, source_target_pairs={{0,1},{1,2},{2,3},{3,4},{4,5},{5,6},{6,7},{7,0},{8,9},{9,10},{10,1... | collective-permute-start | bytes 589832 | tf_op jit(solution)/shard_map/ppermute | solution.py:15
  11.2 10.9 %collective-permute-start.1 = (bf16[1,16,6144]{2,1,0:T(8,128)(2,1)S(1)}, bf16[1,16,6144]{2,1,0:T(8,128)(2,1)S(1)}, u32[]{:S(2)}, u32[]{:S(2)}) collective-permute-start(bf16[1,16,6144]{2,1,0:T(8,128)(2,1)S(1)} %copy-done), channel_id=1, source_target_pairs={{0,7},{1,0},{2,1},{3,2},{4,3},{5,4},{6,5},{7,6},{8,15},{9,8},{10,9... | collective-permute-start | bytes 589832 | tf_op jit(solution)/shard_map/ppermute | solution.py:18
  14.4 55.1 %copy-start.3 = (f32[3072]{0:T(1024)S(1)}, f32[3072]{0:T(1024)}, u32[]{:S(2)}) copy-start(f32[3072]{0:T(1024)} %param.9) | copy-start | bytes 36868
  19.5 10.0 %collective-permute-start.2 = (bf16[1,16,6144]{2,1,0:T(8,128)(2,1)S(1)}, bf16[1,16,6144]{2,1,0:T(8,128)(2,1)S(1)}, u32[]{:S(2)}, u32[]{:S(2)}) collective-permute-start(bf16[1,16,6144]{2,1,0:T(8,128)(2,1)S(1)} %collective-permute-done), channel_id=1, source_target_pairs={{0,1},{1,2},{2,3},{3,4},{4,5},{5,6},{6,7},{7,0},{8,9},{9,10},{10,1... | collective-permute-start | bytes 589832 | tf_op jit(solution)/shard_map/ppermute | solution.py:15
  22.0 10.0 %collective-permute-start.3 = (bf16[1,16,6144]{2,1,0:T(8,128)(2,1)S(1)}, bf16[1,16,6144]{2,1,0:T(8,128)(2,1)S(1)}, u32[]{:S(2)}, u32[]{:S(2)}) collective-permute-start(bf16[1,16,6144]{2,1,0:T(8,128)(2,1)S(1)} %collective-permute-done.1), channel_id=1, source_target_pairs={{0,7},{1,0},{2,1},{3,2},{4,3},{5,4},{6,5},{7,6},{8,15},{9,8},{10,9... | collective-permute-start | bytes 589832 | tf_op jit(solution)/shard_map/ppermute | solution.py:18
  29.5 10.6 %collective-permute-start.4 = (bf16[1,16,6144]{2,1,0:T(8,128)(2,1)S(1)}, bf16[1,16,6144]{2,1,0:T(8,128)(2,1)S(1)}, u32[]{:S(2)}, u32[]{:S(2)}) collective-permute-start(bf16[1,16,6144]{2,1,0:T(8,128)(2,1)S(1)} %collective-permute-done.2), channel_id=1, source_target_pairs={{0,1},{1,2},{2,3},{3,4},{4,5},{5,6},{6,7},{7,0},{8,9},{9,10},{10,1... | collective-permute-start | bytes 589832 | tf_op jit(solution)/shard_map/ppermute | solution.py:15
  32.0 11.2 %collective-permute-start.5 = (bf16[1,16,6144]{2,1,0:T(8,128)(2,1)S(1)}, bf16[1,16,6144]{2,1,0:T(8,128)(2,1)S(1)}, u32[]{:S(2)}, u32[]{:S(2)}) collective-permute-start(bf16[1,16,6144]{2,1,0:T(8,128)(2,1)S(1)} %collective-permute-done.3), channel_id=1, source_target_pairs={{0,7},{1,0},{2,1},{3,2},{4,3},{5,4},{6,5},{7,6},{8,15},{9,8},{10,9... | collective-permute-start | bytes 589832 | tf_op jit(solution)/shard_map/ppermute | solution.py:18
  40.1 10.1 %collective-permute-start.6 = (bf16[1,16,6144]{2,1,0:T(8,128)(2,1)S(1)}, bf16[1,16,6144]{2,1,0:T(8,128)(2,1)S(1)}, u32[]{:S(2)}, u32[]{:S(2)}) collective-permute-start(bf16[1,16,6144]{2,1,0:T(8,128)(2,1)S(1)} %collective-permute-done.4), channel_id=1, source_target_pairs={{0,1},{1,2},{2,3},{3,4},{4,5},{5,6},{6,7},{7,0},{8,9},{9,10},{10,1... | collective-permute-start | bytes 589832 | tf_op jit(solution)/shard_map/ppermute | solution.py:15
  69.5 21.3 %copy-start.1 = (f32[3,3,3072]{2,1,0:T(4,128)S(1)}, f32[3,3,3072]{2,1,0:T(4,128)}, u32[]{:S(2)}) copy-start(f32[3,3,3072]{2,1,0:T(4,128)} %param.10) | copy-start | bytes 331780
  87.3 42.7 %copy-start.4 = (f32[3072]{0:T(1024)S(1)}, f32[3072]{0:T(1024)}, u32[]{:S(2)}) copy-start(f32[3072]{0:T(1024)} %param.11) | copy-start | bytes 36868
  87.5 3.4 %collective-permute-start.7 = (bf16[8,1,3072]{2,1,0:T(2,128)(2,1)S(1)}, bf16[8,1,3072]{2,1,0:T(2,128)(2,1)S(1)}, u32[]{:S(2)}, u32[]{:S(2)}) collective-permute-start(bf16[8,1,3072]{2,1,0:T(2,128)(2,1)S(1)} %get-tuple-element.5), channel_id=1, source_target_pairs={{0,8},{1,9},{2,10},{3,11},{4,12},{5,13},{6,14},{7,15},{16,24},{17,... | collective-permute-start | bytes 147464 | tf_op jit(solution)/shard_map/ppermute | solution.py:30
  89.4 3.2 %collective-permute-start.8 = (bf16[8,1,3072]{2,1,0:T(2,128)(2,1)S(1)}, bf16[8,1,3072]{2,1,0:T(2,128)(2,1)S(1)}, u32[]{:S(2)}, u32[]{:S(2)}) collective-permute-start(bf16[8,1,3072]{2,1,0:T(2,128)(2,1)S(1)} %get-tuple-element.6), channel_id=1, source_target_pairs={{8,0},{9,1},{10,2},{11,3},{12,4},{13,5},{14,6},{15,7},{24,16},{25,... | collective-permute-start | bytes 147464 | tf_op jit(solution)/shard_map/ppermute | solution.py:33
  147.9 75.6 %copy-start.2 = (f32[6144]{0:T(1024)S(1)}, f32[6144]{0:T(1024)}, u32[]{:S(2)}) copy-start(f32[6144]{0:T(1024)} %param.13) | copy-start | bytes 73732
Sparse Core Ops, SparseCore 0:
  8.9 60.4 all-gather.2
  71.0 58.9 all-gather.4
  148.1 75.4 reduce-scatter.1
